TPU v7x, 32 devices: a whole 2x2x4 slice. The times are simulated.
32 devices in a mesh: row: 4 (over y, x), col: 8 (over z, core).
Axes of the slice: x: 2, y: 2, z: 4, core: 2. Of those that a mesh axis runs over, the one named last changes fastest.
Arguments:
- tokens: bfloat16 [1024, 6144], P('col', 'row'), may hold values from -6 to 6
- learning_rate: float32 [1], replicated, may hold values from 0.05 to 0.5
- weight_in: bfloat16 [6144, 24576], P('row', 'col'), may hold values from -0.078125 to 0.078125
- grad_in: bfloat16 [6144, 24576], P('row', 'col'), may hold values from -6 to 6
- moment_in: bfloat16 [6144, 24576], P('row', 'col'), may hold values from -4 to 4
- second_in: bfloat16 [6144, 24576], P('row', 'col'), may hold values from 0.25 to 4
- weight_out: bfloat16 [24576, 6144], P('col', 'row'), may hold values from -0.0390625 to 0.0390625
- grad_out: bfloat16 [24576, 6144], P('col', 'row'), may hold values from -6 to 6
- moment_out: bfloat16 [24576, 6144], P('col', 'row'), may hold values from -4 to 4
- second_out: bfloat16 [24576, 6144], P('col', 'row'), may hold values from 0.25 to 4
Outputs:
- block_out: bfloat16 [1024, 6144], P('col', 'row')
- block_tangent: bfloat16 [1024, 6144], P('col', 'row')
All inputs are finite; a program needn't handle non-finite values.
Results may differ from a plain program's by a relative error of at most 0.025.
Values may be sent and summed in bfloat16 or wider, within the bound.
A program may use at most 192 MiB of HBM per device.

v0:
```python
import math

import jax
import jax.numpy as jnp
from jax import lax
from jax.sharding import PartitionSpec as P

D = 6144
FF = 24576


first_decay = 0.9
second_decay = 0.95
first_fix = 1.0 - 0.9**20
second_fix = 1.0 - 0.95**20
epsilon = 1e-08
gelu_coeff = math.sqrt(2.0 / math.pi)


def adam_direction(grad, moment, second, scale):
    grad_wide = grad.astype(jnp.float32)
    moment_new = first_decay * moment.astype(jnp.float32) + (1.0 - first_decay) * grad_wide
    second_new = (
        second_decay * second.astype(jnp.float32) + (1.0 - second_decay) * grad_wide * grad_wide
    )
    return -scale * (moment_new / first_fix) / (jnp.sqrt(second_new / second_fix) + epsilon)


def activate(hidden_pair, width):
    hidden = hidden_pair[:, :width]
    hidden_tan = hidden_pair[:, width:]
    inner = gelu_coeff * (hidden + 0.044715 * hidden * hidden * hidden)
    shaped = jnp.tanh(inner)
    value = 0.5 * hidden * (1.0 + shaped)
    slope = 0.5 * (1.0 + shaped) + 0.5 * hidden * (1.0 - shaped * shaped) * gelu_coeff * (
        1.0 + 3.0 * 0.044715 * hidden * hidden
    )
    return (value.astype(jnp.bfloat16), (slope * hidden_tan).astype(jnp.bfloat16))


def body(
    tokens,
    learning_rate,
    weight_in,
    grad_in,
    moment_in,
    second_in,
    weight_out,
    grad_out,
    moment_out,
    second_out,
):
    rate = learning_rate[0]
    dir_in = adam_direction(grad_in, moment_in, second_in, 1.0 / math.sqrt(D))
    new_in = (weight_in.astype(jnp.float32) + rate * dir_in).astype(jnp.bfloat16)
    delta_in = dir_in.astype(jnp.bfloat16)
    dir_out = adam_direction(grad_out, moment_out, second_out, 1.0 / math.sqrt(FF))
    new_out = (weight_out.astype(jnp.float32) + rate * dir_out).astype(jnp.bfloat16)
    delta_out = dir_out.astype(jnp.bfloat16)
    local_ff = weight_in.shape[1]
    local_d = weight_out.shape[1]
    piece = lax.all_gather(tokens, "col", axis=0, tiled=True)
    partials = jnp.concatenate(
        [
            jnp.dot(piece, new_in, preferred_element_type=jnp.float32),
            jnp.dot(piece, delta_in, preferred_element_type=jnp.float32),
        ],
        axis=1,
    )
    shares = lax.psum_scatter(
        partials.astype(jnp.bfloat16), "row", scatter_dimension=0, tiled=True
    ).astype(jnp.float32)
    value_part, tangent_part = activate(shares, local_ff)
    value, tangent = (
        lax.all_gather(value_part, "row", axis=0, tiled=True),
        lax.all_gather(tangent_part, "row", axis=0, tiled=True),
    )
    primal = jnp.dot(value, new_out, preferred_element_type=jnp.float32)
    along = jnp.dot(tangent, new_out, preferred_element_type=jnp.float32) + jnp.dot(
        value, delta_out, preferred_element_type=jnp.float32
    )
    result = lax.psum_scatter(
        jnp.concatenate([primal, along], axis=1).astype(jnp.bfloat16),
        "col",
        scatter_dimension=0,
        tiled=True,
    ).astype(jnp.float32)
    return (result[:, :local_d].astype(jnp.bfloat16), result[:, local_d:].astype(jnp.bfloat16))


def solution(mesh):
    return jax.shard_map(
        body,
        mesh=mesh,
        in_specs=(
            P("col", "row"),
            P(),
            P("row", "col"),
            P("row", "col"),
            P("row", "col"),
            P("row", "col"),
            P("col", "row"),
            P("col", "row"),
            P("col", "row"),
            P("col", "row"),
        ),
        out_specs=(P("col", "row"), P("col", "row")),
        check_vma=False,
    )
```

profile of v0, /device:TPU:0, one launch (start us, length us, event | category | flops | bytes accessed | tf_op | source)
XLA Modules:
  0.0 526.7 jit_solution(2493390453388795712)
XLA Ops:
  7.2 0.0 all-gather.4.cloned.1.call-start
  7.2 0.7 all-gather.4.cloned.1.call-update
  7.9 0.0 reduce-scatter.3.cloned.1.call-start
  8.6 42.0 %all-gather.4.cloned.1.call-done = bf16[1024,1536]{1,0:T(8,128)(2,1)} async-done(((bf16[128,1536]{1,0:T(8,128)(2,1)}), bf16[1024,1536]{1,0:T(8,128)(2,1)}) %all-gather.4.cloned.1.call-update) | async-done | bytes 3145744 | tf_op jit(solution)/shard_map/all_gather | solution.py:62
  50.6 0.0 copy-start.1
  50.6 32.9 %convert_bitcast_fusion = bf16[1024,3072]{0,1:T(8,128)(2,1)} fusion(bf16[1024,1536]{1,0:T(8,128)(2,1)} %all-gather.4.cloned.1.call-done, bf16[1536,3072]{1,0:T(8,128)(2,1)} %param.13, bf16[1536,3072]{1,0:T(8,128)(2,1)} %param.15, bf16[1536,3072]{1,0:T(8,128)(2,1)} %param.14), kind=kOutput, calls=%fused_computation.29 | convolution fusion | flops 9737601024 | bytes 37748736 | tf_op jit(solution)/shard_map/dot_general | solution.py:66
  83.5 0.0 copy-done.1
  83.5 0.0 copy-start
  83.5 29.8 %convert_bitcast_fusion.1 = bf16[1024,3072]{0,1:T(8,128)(2,1)} fusion(bf16[1024,1536]{1,0:T(8,128)(2,1)S(1)} %copy-done.1, bf16[1536,3072]{1,0:T(8,128)(2,1)} %param.12, f32[]{:T(128)} %bitcast.12, bf16[1536,3072]{1,0:T(8,128)(2,1)} %param.13, bf16[1536,3072]{1,0:T(8,128)(2,1)} %param.15, bf16[1536,3072]{1,0:T(8,128)(2,1)} %param.14), kind=kOutput, calls=%fused_computation.30 | convolution fusion | flops 9751756800 | bytes 47185924 | tf_op jit(solution)/shard_map/dot_general | solution.py:65
  113.3 0.0 copy-done
  113.3 16.7 %pad_maximum_fusion = bf16[1024,6144]{0,1:T(8,128)(2,1)} fusion(bf16[1024,3072]{0,1:T(8,128)(2,1)S(1)} %copy-done, bf16[1024,3072]{0,1:T(8,128)(2,1)} %convert_bitcast_fusion.1), kind=kLoop, calls=%fused_computation.20 | loop fusion | flops 25165824 | bytes 25165824 | tf_op jit(solution)/shard_map/concatenate | solution.py:63
  130.1 0.0 reduce-scatter.3.cloned.1.call-update
  130.1 0.0 all-gather.8.cloned.1.call-start
  130.1 119.6 %reduce-scatter.3.cloned.1.call-done = bf16[256,6144]{0,1:T(8,128)(2,1)} async-done(((bf16[1024,6144]{0,1:T(8,128)(2,1)}), bf16[256,6144]{0,1:T(8,128)(2,1)}) %reduce-scatter.3.cloned.1.call-update) | async-done | bytes 3145744 | tf_op jit(solution)/shard_map/reduce_scatter | solution.py:70
  249.7 2.4 convert_element_type.56
  252.1 3.4 multiply_convert_fusion
  255.5 0.0 all-gather.8.cloned.1.call-update
  255.6 0.0 all-gather.6.cloned.1.call-start
  255.6 0.5 all-gather.6.cloned.1.call-update
  256.2 0.0 reduce-scatter.5.cloned.1.call-start
  256.2 23.0 %add_convert_fusion = bf16[3072,1536]{1,0:T(8,128)(2,1)} fusion(bf16[3072,1536]{1,0:T(8,128)(2,1)} %param.16, f32[]{:T(128)} %bitcast.13, bf16[3072,1536]{1,0:T(8,128)(2,1)} %param.19, bf16[3072,1536]{1,0:T(8,128)(2,1)} %param.17, bf16[3072,1536]{1,0:T(8,128)(2,1)} %param.18), kind=kLoop, calls=%fused_computation.18 | loop fusion | flops 84934656 | bytes 47185924 | tf_op jit(solution)/shard_map/convert_element_type | solution.py:58
  279.2 46.5 %all-gather.8.cloned.1.call-done = bf16[1024,3072]{0,1:T(8,128)(2,1)} async-done(((bf16[256,3072]{0,1:T(8,128)(2,1)}), bf16[1024,3072]{0,1:T(8,128)(2,1)}) %all-gather.8.cloned.1.call-update) | async-done | bytes 6291472 | tf_op jit(solution)/shard_map/all_gather | solution.py:76
  325.6 15.5 %fusion.35 = f32[1024,1536]{1,0:T(8,128)} fusion(bf16[1024,3072]{0,1:T(8,128)(2,1)} %all-gather.8.cloned.1.call-done, bf16[3072,1536]{1,0:T(8,128)(2,1)} %add_convert_fusion), kind=kOutput, calls=%fused_computation.43 | convolution fusion | flops 9663676416 | bytes 22020096 | tf_op jit(solution)/shard_map/dot_general | solution.py:79
  341.2 56.1 %all-gather.6.cloned.1.call-done = bf16[1024,3072]{0,1:T(8,128)(2,1)} async-done(((bf16[256,3072]{0,1:T(8,128)(2,1)}), bf16[1024,3072]{0,1:T(8,128)(2,1)}) %all-gather.6.cloned.1.call-update) | async-done | bytes 6291472 | tf_op jit(solution)/shard_map/all_gather | solution.py:75
  397.2 14.1 %convolution_convert_fusion = bf16[1024,1536]{1,0:T(8,128)(2,1)S(1)} fusion(bf16[1024,3072]{0,1:T(8,128)(2,1)} %all-gather.6.cloned.1.call-done, bf16[3072,1536]{1,0:T(8,128)(2,1)} %add_convert_fusion), kind=kOutput, calls=%fused_computation.33 | convolution fusion | flops 9665249280 | bytes 18874368 | tf_op jit(solution)/shard_map/dot_general | solution.py:78
  411.4 31.2 %add_convert_fusion.3 = bf16[1024,1536]{1,0:T(8,128)(2,1)} fusion(f32[1024,1536]{1,0:T(8,128)} %fusion.35, bf16[1024,3072]{0,1:T(8,128)(2,1)} %all-gather.6.cloned.1.call-done, bf16[3072,1536]{1,0:T(8,128)(2,1)} %param.17, bf16[3072,1536]{1,0:T(8,128)(2,1)} %param.19, bf16[3072,1536]{1,0:T(8,128)(2,1)} %param.18), kind=kOutput, calls=%fused_computation.28 | convolution fusion | flops 9737601024 | bytes 44040192 | tf_op jit(solution)/shard_map/dot_general | solution.py:79
  442.5 5.3 pad_maximum_fusion.1
  447.8 0.0 reduce-scatter.5.cloned.1.call-update
  447.8 69.9 %reduce-scatter.5.cloned.1.call-done = bf16[128,3072]{1,0:T(8,128)(2,1)} async-done(((bf16[1024,3072]{1,0:T(8,128)(2,1)}), bf16[128,3072]{1,0:T(8,128)(2,1)}) %reduce-scatter.5.cloned.1.call-update) | async-done | bytes 786448 | tf_op jit(solution)/shard_map/reduce_scatter | solution.py:82
  517.7 2.0 fusion.34
Async XLA Ops:
  7.2 43.4 %all-gather.4.cloned.1.call-start = ((), (), s32[]{:S(2)}) async-start(), calls=%async_computation.2 | async-start | bytes 3538944 | tf_op jit(solution)/shard_map/all_gather | solution.py:62
  7.9 241.8 %reduce-scatter.3.cloned.1.call-start = ((), (), s32[]{:S(2)}) async-start(), calls=%async_computation.3 | async-start | bytes 15728640 | tf_op jit(solution)/shard_map/reduce_scatter | solution.py:70
  50.6 32.9 %copy-start.1 = (bf16[1024,1536]{1,0:T(8,128)(2,1)S(1)}, bf16[1024,1536]{1,0:T(8,128)(2,1)}, u32[]{:S(2)}) copy-start(bf16[1024,1536]{1,0:T(8,128)(2,1)} %all-gather.4.cloned.1.call-done) | copy-start | bytes 9437188
  83.5 29.8 %copy-start = (bf16[1024,3072]{0,1:T(8,128)(2,1)S(1)}, bf16[1024,3072]{0,1:T(8,128)(2,1)}, u32[]{:S(2)}) copy-start(bf16[1024,3072]{0,1:T(8,128)(2,1)} %convert_bitcast_fusion) | copy-start | bytes 18874372
  130.1 195.6 %all-gather.8.cloned.1.call-start = ((), (), s32[]{:S(2)}) async-start(), calls=%async_computation.5 | async-start | bytes 7864320 | tf_op jit(solution)/shard_map/all_gather | solution.py:76
  255.6 141.7 %all-gather.6.cloned.1.call-start = ((), (), s32[]{:S(2)}) async-start(), calls=%async_computation.4 | async-start | bytes 7864320 | tf_op jit(solution)/shard_map/all_gather | solution.py:75
  256.2 261.6 %reduce-scatter.5.cloned.1.call-start = ((), (), s32[]{:S(2)}) async-start(), calls=%async_computation.6 | async-start | bytes 7077888 | tf_op jit(solution)/shard_map/reduce_scatter | solution.py:82
Sparse Core Ops, SparseCore 0:
  9.6 40.9 all-gather.3
  130.2 119.4 reduce-scatter.2
  255.7 69.8 all-gather.7
  327.3 69.8 all-gather.5
  447.9 69.7 reduce-scatter.4
where the time goes:
time: 535 us; the launch traced here: 527 us
  waiting for transfers between devices  335 us (63%)
  matrix products  124 us (23%)
  other arithmetic  50.8 us (9%)
  between operations  14.9 us (3%)
    reduce_scatter x1, waiting for transfers between devices, body(): lax.psum_scatter(partials.astype(jnp.bfloat16), 'row', scatter_dimension=...  120 us
    reduce_scatter x1, waiting for transfers between devices, body(): lax.psum_scatter(jnp.concatenate([primal, along], axis=1).astype(jnp.bflo...  69.9 us
    all_gather x1, waiting for transfers between devices, body(): lax.all_gather(value_part, 'row', axis=0, tiled=True)  56.1 us
    all_gather x1, waiting for transfers between devices, body(): lax.all_gather(tangent_part, 'row', axis=0, tiled=True)  46.5 us
    all_gather x1, waiting for transfers between devices, body(): piece = lax.all_gather(tokens, 'col', axis=0, tiled=True)  42 us
    dot_general x1, matrix products, body(): jnp.dot(piece, delta_in, preferred_element_type=jnp.float32)  32.9 us
    dot_general x1, matrix products, body(): jnp.dot(value, delta_out, preferred_element_type=jnp.float32)  31.2 us
    dot_general x1, matrix products, body(): jnp.dot(piece, new_in, preferred_element_type=jnp.float32)  29.8 us
  transfers between devices with their start and end apart: 5, of which 5 were waited for; matrix products, arithmetic and copies ran while one was open for 7% of the time, Pallas kernels for 0%

commit v1 on v0

v1 whole, which is shorter than its diff:
```python
import math

import jax
import jax.numpy as jnp
from jax import lax
from jax.sharding import PartitionSpec as P


first_decay = 0.9
second_decay = 0.95
first_fix = 1.0 - 0.9**20
second_fix = 1.0 - 0.95**20
epsilon = 1e-08
gelu_coeff = math.sqrt(2.0 / math.pi)

MOST_CHUNKS = 4
PIECES = 2


def adam_direction(grad, moment, second, scale):
    grad_wide = grad.astype(jnp.float32)
    moment_new = first_decay * moment.astype(jnp.float32) + (1.0 - first_decay) * grad_wide
    second_new = (
        second_decay * second.astype(jnp.float32) + (1.0 - second_decay) * grad_wide * grad_wide
    )
    return -scale * (moment_new / first_fix) / (jnp.sqrt(second_new / second_fix) + epsilon)


def adam(weight, grad, moment, second, rate, fan_in):
    direction = adam_direction(grad, moment, second, 1.0 / math.sqrt(fan_in))
    new = (weight.astype(jnp.float32) + rate * direction).astype(jnp.bfloat16)
    return lax.optimization_barrier((new, direction.astype(jnp.bfloat16)))


def activate(hidden, hidden_tan):
    inner = gelu_coeff * (hidden + 0.044715 * hidden * hidden * hidden)
    shaped = jnp.tanh(inner)
    value = 0.5 * hidden * (1.0 + shaped)
    slope = 0.5 * (1.0 + shaped) + 0.5 * hidden * (1.0 - shaped * shaped) * gelu_coeff * (
        1.0 + 3.0 * 0.044715 * hidden * hidden
    )
    return (value.astype(jnp.bfloat16), (slope * hidden_tan).astype(jnp.bfloat16))


def add(a, b):
    return a.astype(jnp.float32) + b.astype(jnp.float32)


def swap(block, axis, n, bit):
    return lax.ppermute(block, axis, [(i, i ^ (1 << bit)) for i in range(n)])


def shifted(block, n_col, shift):
    return lax.ppermute(block, "col", [(i, (i + 2 * shift) % n_col) for i in range(n_col)])


def scatter_row(part, n_row, order):
    me = lax.axis_index("row")
    bits = sorted(order, reverse=True)
    blocks = part.reshape((2,) * len(bits) + part.shape[1:])
    for step, bit in enumerate(order):
        place = bits.index(bit)
        bits.remove(bit)
        mine = lax.rem(lax.div(me, 1 << bit), 2)
        keep = lax.dynamic_index_in_dim(blocks, mine, place, False)
        give = lax.dynamic_index_in_dim(blocks, 1 - mine, place, False)
        blocks = add(keep, swap(give, "row", n_row, bit))
        if step < len(order) - 1:
            blocks = blocks.astype(jnp.bfloat16)
    return blocks


def gather_row(block, n_row, order):
    held = block[None]
    done = []
    for bit in order:
        arrived = swap(held, "row", n_row, bit)
        held = jnp.concatenate([held, arrived], axis=0)
        done.append(bit)
    shape = (2,) * len(done) + block.shape
    held = held.reshape(shape)
    axes = done[::-1]
    perm = [axes.index(b) for b in sorted(done, reverse=True)]
    held = held.transpose(perm + list(range(len(done), len(shape))))
    return held.reshape((n_row,) + block.shape)


def gather_col(block, n_col):
    n_chip = n_col // 2
    me = lax.axis_index("col")
    core, chip = lax.rem(me, 2), lax.div(me, 2)
    held = [block]
    for shift in range(1, n_chip):
        held.append(shifted(block, n_col, shift))
    stacked = jnp.stack(held[::-1] * 2)
    line = lax.dynamic_slice_in_dim(stacked, n_chip - 1 - chip, n_chip, 0)
    other = swap(line, "col", n_col, 0)
    first = jnp.where(core == 0, line, other)
    second = jnp.where(core == 0, other, line)
    return jnp.stack([first, second], axis=1).reshape((n_col,) + block.shape)


def core_sum(part, n_col):
    core = lax.rem(lax.axis_index("col"), 2)
    blocks = part.reshape((n_col // 2, 2) + part.shape[1:])
    mine = lax.dynamic_index_in_dim(blocks, core, 1, False)
    other = lax.dynamic_index_in_dim(blocks, 1 - core, 1, False)
    return add(mine, swap(other, "col", n_col, 0)).astype(jnp.bfloat16)


def line_send(pair, n_col):
    n_chip = n_col // 2
    chip = lax.div(lax.axis_index("col"), 2)
    terms = [lax.dynamic_index_in_dim(pair, chip, 0, False)]
    for shift in range(1, n_chip):
        block = lax.dynamic_index_in_dim(pair, lax.rem(chip + shift, n_chip), 0, False)
        terms.append(shifted(block, n_col, shift))
    return terms


def chunk_count(local_tokens, n_row):
    return max(1, min(MOST_CHUNKS, local_tokens // n_row))


def make_body(n_row, n_col):
    up = list(range(n_row.bit_length() - 1))
    down = up[::-1]

    def body(
        tokens,
        learning_rate,
        weight_in,
        grad_in,
        moment_in,
        second_in,
        weight_out,
        grad_out,
        moment_out,
        second_out,
    ):
        rate = learning_rate[0]
        depth, local_ff = weight_in.shape
        local_d = weight_out.shape[1]
        chunks = chunk_count(tokens.shape[0], n_row)
        small = tokens.shape[0] // (chunks * n_row)
        per_piece = chunks // PIECES
        held = []
        for k in range(PIECES):
            rows = tokens.shape[0] // PIECES
            piece = gather_col(tokens[k * rows : (k + 1) * rows], n_col)
            piece = piece.reshape(n_col, per_piece, n_row, small, depth)
            piece = piece.transpose(1, 2, 0, 3, 4).reshape(per_piece, -1, depth)
            held.extend(piece[i] for i in range(per_piece))
        new_in, delta_in = adam(
            weight_in, grad_in, moment_in, second_in, rate, depth * n_row
        )
        shares = []
        for c in range(chunks):
            pair = []
            for w, order in ((new_in, up), (delta_in, down)):
                part = jnp.dot(held[c], w, preferred_element_type=jnp.float32)
                part = part.astype(jnp.bfloat16).reshape(n_row, -1, local_ff)
                pair.append(scatter_row(part, n_row, order))
            shares.append(pair)
        new_out, delta_out = adam(
            weight_out, grad_out, moment_out, second_out, rate, weight_out.shape[0] * n_col
        )
        lines = []
        for c in range(chunks):
            value, tangent = activate(*shares[c])
            value = gather_row(value, n_row, down).reshape(-1, local_ff)
            tangent = gather_row(tangent, n_row, up).reshape(-1, local_ff)
            primal = jnp.dot(value, new_out, preferred_element_type=jnp.float32)
            along = jnp.dot(tangent, new_out, preferred_element_type=jnp.float32) + jnp.dot(
                value, delta_out, preferred_element_type=jnp.float32
            )
            part = jnp.concatenate(
                [primal.astype(jnp.bfloat16), along.astype(jnp.bfloat16)], axis=1
            )
            part = part.reshape(n_row, n_col, small, 2 * local_d).transpose(1, 0, 2, 3)
            part = part.reshape(n_col, n_row * small, 2 * local_d)
            pair = core_sum(part, n_col)
            lines.append(line_send(pair, n_col))
        me = lax.axis_index("row")
        places = jnp.arange(n_row) ^ me
        results = []
        for terms in lines:
            total = terms[0].astype(jnp.float32)
            for term in terms[1:]:
                total += term.astype(jnp.float32)
            total = total.astype(jnp.bfloat16).reshape(n_row, small, -1)
            results.append(jnp.take(total, places, axis=0, mode="clip").reshape(n_row * small, -1))
        result = jnp.concatenate(results, axis=0)
        return (result[:, :local_d], result[:, local_d:])

    return body


def solution(mesh):
    n_row, n_col = mesh.shape["row"], mesh.shape["col"]
    return jax.shard_map(
        make_body(n_row, n_col),
        mesh=mesh,
        in_specs=(
            P("col", "row"),
            P(),
            P("row", "col"),
            P("row", "col"),
            P("row", "col"),
            P("row", "col"),
            P("col", "row"),
            P("col", "row"),
            P("col", "row"),
            P("col", "row"),
        ),
        out_specs=(P("col", "row"), P("col", "row")),
        check_vma=False,
    )
```

time: 535 us -> 424 us (0.79)
  waiting for transfers between devices: 335 us -> 192 us
  starting transfers between devices: 0.2 us -> 82 us
  matrix products: 124 us -> 59 us
  local copies, waits for them, and re-layouts: 2.05 us -> 20.2 us
  between operations: 14.9 us -> 3.09 us
  other arithmetic: 50.8 us -> 60.9 us
    ppermute x0 -> x56, waiting for transfers between devices: none -> 192 us  [the longest x38 144 us: swap(): return lax.ppermute(block, axis, [(i, i ^ 1 << bit) for i in range(n)])]
    reduce_scatter x2 -> x0, waiting for transfers between devices: 190 us -> none  [the longest x1 120 us: body(): lax.psum_scatter(partials.astype(jnp.bfloat16), 'row', scatter_dimension=...]
    all_gather x3 -> x0, waiting for transfers between devices: 145 us -> none  [the longest x1 56.1 us: body(): lax.all_gather(value_part, 'row', axis=0, tiled=True)]
    ppermute x0 -> x56, starting transfers between devices: none -> 82 us  [the longest x38 43.9 us: swap(): return lax.ppermute(block, axis, [(i, i ^ 1 << bit) for i in range(n)])]
    dot_general x2 -> x8, matrix products: 62.7 us -> 25.1 us  [body(): part = jnp.dot(held[c], w, preferred_element_type=jnp.float32)]
    convert_element_type x3 -> x14, other arithmetic: 28.8 us -> 52.7 us  [the longest x2 50.4 us: adam(): return lax.optimization_barrier((new, direction.astype(jnp.bfloat16)))]
    concatenate x2 -> x21, other arithmetic: 22 us -> 2.64 us  [the longest x16 1.83 us: gather_row(): held = jnp.concatenate([held, arrived], axis=0)]
    dot_general x1 -> x4, matrix products: 31.2 us -> 12.7 us  [body(): jnp.dot(value, delta_out, preferred_element_type=jnp.float32)]
  transfers between devices with their start and end apart: 5 -> 56, of which waited for: 5 -> 21; matrix products, arithmetic and copies ran while one was open for 7% -> 28% of each run, Pallas kernels for 0% -> 0%
where the time goes in v1:
time: 424 us; the launch traced here: 417 us
  waiting for transfers between devices  192 us (45%)
  starting transfers between devices  82 us (19%)
  other arithmetic  60.9 us (14%)
  matrix products  59 us (14%)
  local copies, waits for them, and re-layouts  20.2 us (5%)
    ppermute x38, waiting for transfers between devices, swap(): return lax.ppermute(block, axis, [(i, i ^ 1 << bit) for i in range(n)])  144 us
    convert_element_type x2, other arithmetic, adam(): return lax.optimization_barrier((new, direction.astype(jnp.bfloat16)))  50.4 us
    ppermute x18, waiting for transfers between devices, shifted(): lax.ppermute(block, 'col', [(i, (i + 2 * shift) % n_col) for i in range(n...  47.7 us
    ppermute x38, starting transfers between devices, swap(): return lax.ppermute(block, axis, [(i, i ^ 1 << bit) for i in range(n)])  43.9 us
    ppermute x18, starting transfers between devices, shifted(): lax.ppermute(block, 'col', [(i, (i + 2 * shift) % n_col) for i in range(n...  38.1 us
    dot_general x8, matrix products, body(): part = jnp.dot(held[c], w, preferred_element_type=jnp.float32)  25.1 us
    dot_general x4, matrix products, body(): jnp.dot(value, delta_out, preferred_element_type=jnp.float32)  12.7 us
    unnamed x48, local copies, waits for them, and re-layouts  11.6 us
  transfers between devices with their start and end apart: 56, of which 21 were waited for; matrix products, arithmetic and copies ran while one was open for 28% of the time, Pallas kernels for 0%

profile of v1, /device:TPU:0, one launch (start us, length us, event | category | flops | bytes accessed | tf_op | source)
XLA Modules:
  0.0 417.2 jit_solution(17137700383266449601)
XLA Ops:
  2.4 3.1 collective-permute-start.2
  5.5 2.6 collective-permute-start.1
  10.1 3.1 collective-permute-start.28
  13.9 25.1 %fusion.83 = (bf16[1536,3072]{1,0:T(8,128)(2,1)}, bf16[1536,3072]{1,0:T(8,128)(2,1)}) fusion(bf16[1536,3072]{1,0:T(8,128)(2,1)} %param.15, bf16[1536,3072]{1,0:T(8,128)(2,1)} %param.13, bf16[1536,3072]{1,0:T(8,128)(2,1)} %param.14, f32[]{:T(128)} %bitcast.331, bf16[1536,3072]{1,0:T(8,128)(2,1)} %param.12), kind=kLoop, calls=%fused_computation.224 | loop fusion | flops 89653248 | bytes 56623108 | tf_op jit(solution)/shard_map/convert_element_type | solution.py:32
  40.6 7.3 %collective-permute-done.29 = bf16[64,1536]{1,0:T(8,128)(2,1)S(1)} collective-permute-done((bf16[64,1536]{1,0:T(8,128)(2,1)}, bf16[64,1536]{1,0:T(8,128)(2,1)S(1)}, u32[]{:S(2)}, u32[]{:S(2)}) %collective-permute-start.29) | collective-permute-done | bytes 196640 | tf_op jit(solution)/shard_map/ppermute | solution.py:54
  55.7 25.3 %fusion.82 = (bf16[3072,1536]{1,0:T(8,128)(2,1)}, bf16[3072,1536]{1,0:T(8,128)(2,1)}) fusion(bf16[3072,1536]{1,0:T(8,128)(2,1)} %param.19, bf16[3072,1536]{1,0:T(8,128)(2,1)} %param.17, bf16[3072,1536]{1,0:T(8,128)(2,1)} %param.18, f32[]{:T(128)} %bitcast.332, bf16[3072,1536]{1,0:T(8,128)(2,1)} %param.16), kind=kLoop, calls=%fused_computation.223 | loop fusion | flops 89653248 | bytes 56623108 | tf_op jit(solution)/shard_map/convert_element_type | solution.py:32
  84.1 6.4 %convolution_convert_fusion.1 = bf16[256,3072]{1,0:T(8,128)(2,1)S(1)} fusion(bf16[256,1536]{1,0:T(8,128)(2,1)S(1)} %bitcast.395, bf16[1536,3072]{1,0:T(8,128)(2,1)} %get-tuple-element.6), kind=kOutput, calls=%fused_computation.25 | convolution fusion | flops 2416705536 | bytes 11796480 | tf_op jit(solution)/shard_map/dot_general | solution.py:161
  90.6 2.6 convolution_convert_fusion
  93.3 2.6 convolution_convert_fusion.3
  95.9 2.6 convolution_convert_fusion.2
  99.0 2.6 convolution_convert_fusion.7
  101.6 3.0 convolution_convert_fusion.6
  104.7 2.6 convolution_convert_fusion.5
  107.3 2.6 convolution_convert_fusion.4
  116.3 14.2 %collective-permute-done.48 = bf16[2,64,3072]{2,1,0:T(8,128)(2,1)S(1)} collective-permute-done((bf16[2,64,3072]{2,1,0:T(8,128)(2,1)S(1)}, bf16[2,64,3072]{2,1,0:T(8,128)(2,1)S(1)}, u32[]{:S(2)}, u32[]{:S(2)}) %collective-permute-start.48) | collective-permute-done | bytes 786464 | tf_op jit(solution)/shard_map/ppermute | solution.py:50
  132.2 15.1 %collective-permute-done.36 = bf16[2,64,3072]{2,1,0:T(8,128)(2,1)S(1)} collective-permute-done((bf16[2,64,3072]{2,1,0:T(8,128)(2,1)S(1)}, bf16[2,64,3072]{2,1,0:T(8,128)(2,1)S(1)}, u32[]{:S(2)}, u32[]{:S(2)}) %collective-permute-start.36) | collective-permute-done | bytes 786464 | tf_op jit(solution)/shard_map/ppermute | solution.py:50
  151.7 12.5 %collective-permute-done.20 = bf16[2,64,3072]{2,1,0:T(8,128)(2,1)S(1)} collective-permute-done((bf16[2,64,3072]{2,1,0:T(8,128)(2,1)S(1)}, bf16[2,64,3072]{2,1,0:T(8,128)(2,1)S(1)}, u32[]{:S(2)}, u32[]{:S(2)}) %collective-permute-start.20) | collective-permute-done | bytes 786464 | tf_op jit(solution)/shard_map/ppermute | solution.py:50
  165.9 15.1 %collective-permute-done.8 = bf16[2,64,3072]{2,1,0:T(8,128)(2,1)S(1)} collective-permute-done((bf16[2,64,3072]{2,1,0:T(8,128)(2,1)S(1)}, bf16[2,64,3072]{2,1,0:T(8,128)(2,1)S(1)}, u32[]{:S(2)}, u32[]{:S(2)}) %collective-permute-start.8) | collective-permute-done | bytes 786464 | tf_op jit(solution)/shard_map/ppermute | solution.py:50
  186.4 6.6 %collective-permute-done.49 = bf16[64,3072]{1,0:T(8,128)(2,1)S(1)} collective-permute-done((bf16[64,3072]{1,0:T(8,128)(2,1)S(1)}, bf16[64,3072]{1,0:T(8,128)(2,1)S(1)}, u32[]{:S(2)}, u32[]{:S(2)}) %collective-permute-start.49) | collective-permute-done | bytes 393248 | tf_op jit(solution)/shard_map/ppermute | solution.py:50
  196.7 4.7 %collective-permute-done.37 = bf16[64,3072]{1,0:T(8,128)(2,1)S(1)} collective-permute-done((bf16[64,3072]{1,0:T(8,128)(2,1)S(1)}, bf16[64,3072]{1,0:T(8,128)(2,1)S(1)}, u32[]{:S(2)}, u32[]{:S(2)}) %collective-permute-start.37) | collective-permute-done | bytes 393248 | tf_op jit(solution)/shard_map/ppermute | solution.py:50
  205.2 13.1 %collective-permute-done.9 = bf16[64,3072]{1,0:T(8,128)(2,1)S(1)} collective-permute-done((bf16[64,3072]{1,0:T(8,128)(2,1)S(1)}, bf16[64,3072]{1,0:T(8,128)(2,1)S(1)}, u32[]{:S(2)}, u32[]{:S(2)}) %collective-permute-start.9) | collective-permute-done | bytes 393248 | tf_op jit(solution)/shard_map/ppermute | solution.py:50
  224.0 6.3 %collective-permute-done.46 = bf16[1,64,3072]{2,1,0:T(8,128)(2,1)S(1)} collective-permute-done((bf16[1,64,3072]{2,1,0:T(8,128)(2,1)S(1)}, bf16[1,64,3072]{2,1,0:T(8,128)(2,1)S(1)}, u32[]{:S(2)}, u32[]{:S(2)}) %collective-permute-start.46) | collective-permute-done | bytes 393248 | tf_op jit(solution)/shard_map/ppermute | solution.py:50
  233.5 5.2 %collective-permute-done.34 = bf16[1,64,3072]{2,1,0:T(8,128)(2,1)S(1)} collective-permute-done((bf16[1,64,3072]{2,1,0:T(8,128)(2,1)S(1)}, bf16[1,64,3072]{2,1,0:T(8,128)(2,1)S(1)}, u32[]{:S(2)}, u32[]{:S(2)}) %collective-permute-start.34) | collective-permute-done | bytes 393248 | tf_op jit(solution)/shard_map/ppermute | solution.py:50
  241.0 6.2 %collective-permute-done.6 = bf16[1,64,3072]{2,1,0:T(8,128)(2,1)S(1)} collective-permute-done((bf16[1,64,3072]{2,1,0:T(8,128)(2,1)S(1)}, bf16[1,64,3072]{2,1,0:T(8,128)(2,1)S(1)}, u32[]{:S(2)}, u32[]{:S(2)}) %collective-permute-start.6) | collective-permute-done | bytes 393248 | tf_op jit(solution)/shard_map/ppermute | solution.py:50
  250.4 5.2 %collective-permute-done.18 = bf16[1,64,3072]{2,1,0:T(8,128)(2,1)S(1)} collective-permute-done((bf16[1,64,3072]{2,1,0:T(8,128)(2,1)S(1)}, bf16[1,64,3072]{2,1,0:T(8,128)(2,1)S(1)}, u32[]{:S(2)}, u32[]{:S(2)}) %collective-permute-start.18) | collective-permute-done | bytes 393248 | tf_op jit(solution)/shard_map/ppermute | solution.py:50
  257.8 11.0 %collective-permute-done.47 = bf16[2,64,3072]{2,1,0:T(8,128)(2,1)S(1)} collective-permute-done((bf16[2,64,3072]{2,1,0:T(8,128)(2,1)S(1)}, bf16[2,64,3072]{2,1,0:T(8,128)(2,1)S(1)}, u32[]{:S(2)}, u32[]{:S(2)}) %collective-permute-start.47) | collective-permute-done | bytes 786464 | tf_op jit(solution)/shard_map/ppermute | solution.py:50
  270.6 15.1 %collective-permute-done.35 = bf16[2,64,3072]{2,1,0:T(8,128)(2,1)S(1)} collective-permute-done((bf16[2,64,3072]{2,1,0:T(8,128)(2,1)S(1)}, bf16[2,64,3072]{2,1,0:T(8,128)(2,1)S(1)}, u32[]{:S(2)}, u32[]{:S(2)}) %collective-permute-start.35) | collective-permute-done | bytes 786464 | tf_op jit(solution)/shard_map/ppermute | solution.py:50
  287.5 12.4 %collective-permute-done.7 = bf16[2,64,3072]{2,1,0:T(8,128)(2,1)S(1)} collective-permute-done((bf16[2,64,3072]{2,1,0:T(8,128)(2,1)S(1)}, bf16[2,64,3072]{2,1,0:T(8,128)(2,1)S(1)}, u32[]{:S(2)}, u32[]{:S(2)}) %collective-permute-start.7) | collective-permute-done | bytes 786464 | tf_op jit(solution)/shard_map/ppermute | solution.py:50
  301.7 2.6 convolution_convert_fusion.8
  305.1 3.7 fusion.91
  308.9 3.8 fusion.88
  312.6 2.6 convolution_convert_fusion.11
  316.9 2.6 convolution_convert_fusion.10
  321.0 2.8 fusion.14
  326.9 2.6 fusion.15
  330.0 2.6 convolution_convert_fusion.9
  334.0 2.6 fusion.17
  336.8 2.6 fusion.90
  339.5 2.9 fusion.16
  344.6 3.8 collective-permute-start.15
  349.7 3.2 collective-permute-start.27
  354.2 3.9 collective-permute-start.26
  360.6 9.6 %collective-permute-done.14 = bf16[32,3072]{1,0:T(8,128)(2,1)S(1)} collective-permute-done((bf16[32,3072]{1,0:T(8,128)(2,1)S(1)}, bf16[32,3072]{1,0:T(8,128)(2,1)S(1)}, u32[]{:S(2)}, u32[]{:S(2)}) %collective-permute-start.14) | collective-permute-done | bytes 196640 | tf_op jit(solution)/shard_map/ppermute | solution.py:54
  370.3 7.2 %collective-permute-start.42 = (bf16[32,3072]{1,0:T(8,128)(2,1)S(1)}, bf16[32,3072]{1,0:T(8,128)(2,1)S(1)}, u32[]{:S(2)}, u32[]{:S(2)}) collective-permute-start(bf16[32,3072]{1,0:T(8,128)(2,1)S(1)} %get-tuple-element.40), channel_id=1, source_target_pairs={{0,4},{1,5},{2,6},{3,7},{4,0},{5,1},{6,2},{7,3},{8,12},{9,13},{10,... | collective-permute-start | bytes 589832 | tf_op jit(solution)/shard_map/ppermute | solution.py:54
  377.5 5.8 %collective-permute-start.53 = (bf16[32,3072]{1,0:T(8,128)(2,1)S(1)}, bf16[32,3072]{1,0:T(8,128)(2,1)S(1)}, u32[]{:S(2)}, u32[]{:S(2)}) collective-permute-start(bf16[32,3072]{1,0:T(8,128)(2,1)S(1)} %get-tuple-element.41), channel_id=1, source_target_pairs={{0,2},{1,3},{2,4},{3,5},{4,6},{5,7},{6,0},{7,1},{8,10},{9,11},{10,... | collective-permute-start | bytes 589832 | tf_op jit(solution)/shard_map/ppermute | solution.py:54
  383.3 11.7 %collective-permute-done.26 = bf16[32,3072]{1,0:T(8,128)(2,1)S(1)} collective-permute-done((bf16[32,3072]{1,0:T(8,128)(2,1)S(1)}, bf16[32,3072]{1,0:T(8,128)(2,1)S(1)}, u32[]{:S(2)}, u32[]{:S(2)}) %collective-permute-start.26) | collective-permute-done | bytes 196640 | tf_op jit(solution)/shard_map/ppermute | solution.py:54
  395.2 12.4 %collective-permute-done.42 = bf16[32,3072]{1,0:T(8,128)(2,1)S(1)} collective-permute-done((bf16[32,3072]{1,0:T(8,128)(2,1)S(1)}, bf16[32,3072]{1,0:T(8,128)(2,1)S(1)}, u32[]{:S(2)}, u32[]{:S(2)}) %collective-permute-start.42) | collective-permute-done | bytes 196640 | tf_op jit(solution)/shard_map/ppermute | solution.py:54
  409.4 5.6 %collective-permute-done.54 = bf16[32,3072]{1,0:T(8,128)(2,1)S(1)} collective-permute-done((bf16[32,3072]{1,0:T(8,128)(2,1)S(1)}, bf16[32,3072]{1,0:T(8,128)(2,1)S(1)}, u32[]{:S(2)}, u32[]{:S(2)}) %collective-permute-start.54) | collective-permute-done | bytes 196640 | tf_op jit(solution)/shard_map/ppermute | solution.py:54
  (233 shorter events, 85.3 us)
Async XLA Ops:
  2.4 47.4 %collective-permute-start.2 = (bf16[64,1536]{1,0:T(8,128)(2,1)}, bf16[64,1536]{1,0:T(8,128)(2,1)}, u32[]{:S(2)}, u32[]{:S(2)}) collective-permute-start(bf16[64,1536]{1,0:T(8,128)(2,1)} %get-tuple-element.48), channel_id=1, source_target_pairs={{0,2},{1,3},{2,4},{3,5},{4,6},{5,7},{6,0},{7,1},{8,10},{9,11},{10,... | collective-permute-start | bytes 589832 | tf_op jit(solution)/shard_map/ppermute | solution.py:54
  5.5 43.4 %collective-permute-start.1 = (bf16[64,1536]{1,0:T(8,128)(2,1)}, bf16[64,1536]{1,0:T(8,128)(2,1)}, u32[]{:S(2)}, u32[]{:S(2)}) collective-permute-start(bf16[64,1536]{1,0:T(8,128)(2,1)} %get-tuple-element.48), channel_id=1, source_target_pairs={{0,4},{1,5},{2,6},{3,7},{4,0},{5,1},{6,2},{7,3},{8,12},{9,13},{10,... | collective-permute-start | bytes 589832 | tf_op jit(solution)/shard_map/ppermute | solution.py:54
  8.1 31.6 %collective-permute-start = (bf16[64,1536]{1,0:T(8,128)(2,1)}, bf16[64,1536]{1,0:T(8,128)(2,1)}, u32[]{:S(2)}, u32[]{:S(2)}) collective-permute-start(bf16[64,1536]{1,0:T(8,128)(2,1)} %get-tuple-element.48), channel_id=1, source_target_pairs={{0,6},{1,7},{2,0},{3,1},{4,2},{5,3},{6,4},{7,5},{8,14},{9,15},{10,... | collective-permute-start | bytes 589832 | tf_op jit(solution)/shard_map/ppermute | solution.py:54
  9.4 38.5 %collective-permute-start.30 = (bf16[64,1536]{1,0:T(8,128)(2,1)}, bf16[64,1536]{1,0:T(8,128)(2,1)}, u32[]{:S(2)}, u32[]{:S(2)}) collective-permute-start(bf16[64,1536]{1,0:T(8,128)(2,1)} %get-tuple-element.49), channel_id=1, source_target_pairs={{0,2},{1,3},{2,4},{3,5},{4,6},{5,7},{6,0},{7,1},{8,10},{9,11},{10,... | collective-permute-start | bytes 589832 | tf_op jit(solution)/shard_map/ppermute | solution.py:54
  10.1 28.9 %collective-permute-start.28 = (bf16[64,1536]{1,0:T(8,128)(2,1)}, bf16[64,1536]{1,0:T(8,128)(2,1)S(1)}, u32[]{:S(2)}, u32[]{:S(2)}) collective-permute-start(bf16[64,1536]{1,0:T(8,128)(2,1)} %get-tuple-element.49), channel_id=1, source_target_pairs={{0,6},{1,7},{2,0},{3,1},{4,2},{5,3},{6,4},{7,5},{8,14},{9,15},{10,... | collective-permute-start | bytes 589832 | tf_op jit(solution)/shard_map/ppermute | solution.py:54
  55.7 26.7 %collective-permute-start.31 = (bf16[4,64,1536]{2,1,0:T(8,128)(2,1)}, bf16[4,64,1536]{2,1,0:T(8,128)(2,1)}, u32[]{:S(2)}, u32[]{:S(2)}) collective-permute-start(bf16[4,64,1536]{2,1,0:T(8,128)(2,1)} %constant_dynamic-slice_fusion), channel_id=1, source_target_pairs={{0,1},{1,0},{2,3},{3,2},{4,5},{5,4},{6,7},{7,6},{8,9},{9,8},{10,11... | collective-permute-start | bytes 2359304 | tf_op jit(solution)/shard_map/ppermute | solution.py:50
  81.7 16.8 %collective-permute-start.3 = (bf16[4,64,1536]{2,1,0:T(8,128)(2,1)S(1)}, bf16[4,64,1536]{2,1,0:T(8,128)(2,1)S(1)}, u32[]{:S(2)}, u32[]{:S(2)}) collective-permute-start(bf16[4,64,1536]{2,1,0:T(8,128)(2,1)S(1)} %constant_dynamic-slice_fusion.1), channel_id=1, source_target_pairs={{0,1},{1,0},{2,3},{3,2},{4,5},{5,4},{6,7},{7,6},{8,9},{9,8},{10,11... | collective-permute-start | bytes 2359304 | tf_op jit(solution)/shard_map/ppermute | solution.py:50
  110.0 20.5 %collective-permute-start.48 = (bf16[2,64,3072]{2,1,0:T(8,128)(2,1)S(1)}, bf16[2,64,3072]{2,1,0:T(8,128)(2,1)S(1)}, u32[]{:S(2)}, u32[]{:S(2)}) collective-permute-start(bf16[2,64,3072]{2,1,0:T(8,128)(2,1)S(1)} %dynamic-slice_bitcast_fusion.1), channel_id=1, source_target_pairs={{0,16},{8,24},{16,0},{24,8},{1,17},{9,25},{17,1},{25,9},{2,18},{10... | collective-permute-start | bytes 2359304 | tf_op jit(solution)/shard_map/ppermute | solution.py:50
  111.6 37.4 %collective-permute-start.44 = (bf16[2,64,3072]{2,1,0:T(8,128)(2,1)S(1)}, bf16[2,64,3072]{2,1,0:T(8,128)(2,1)S(1)}, u32[]{:S(2)}, u32[]{:S(2)}) collective-permute-start(bf16[2,64,3072]{2,1,0:T(8,128)(2,1)S(1)} %dynamic-slice_bitcast_fusion.2), channel_id=1, source_target_pairs={{0,8},{8,0},{16,24},{24,16},{1,9},{9,1},{17,25},{25,17},{2,10},{10... | collective-permute-start | bytes 2359304 | tf_op jit(solution)/shard_map/ppermute | solution.py:50
  113.3 34.0 %collective-permute-start.36 = (bf16[2,64,3072]{2,1,0:T(8,128)(2,1)S(1)}, bf16[2,64,3072]{2,1,0:T(8,128)(2,1)S(1)}, u32[]{:S(2)}, u32[]{:S(2)}) collective-permute-start(bf16[2,64,3072]{2,1,0:T(8,128)(2,1)S(1)} %dynamic-slice_bitcast_fusion.4), channel_id=1, source_target_pairs={{0,16},{8,24},{16,0},{24,8},{1,17},{9,25},{17,1},{25,9},{2,18},{10... | collective-permute-start | bytes 2359304 | tf_op jit(solution)/shard_map/ppermute | solution.py:50
  113.9 36.0 %collective-permute-start.32 = (bf16[2,64,3072]{2,1,0:T(8,128)(2,1)S(1)}, bf16[2,64,3072]{2,1,0:T(8,128)(2,1)S(1)}, u32[]{:S(2)}, u32[]{:S(2)}) collective-permute-start(bf16[2,64,3072]{2,1,0:T(8,128)(2,1)S(1)} %dynamic-slice_bitcast_fusion.5), channel_id=1, source_target_pairs={{0,8},{8,0},{16,24},{24,16},{1,9},{9,1},{17,25},{25,17},{2,10},{10... | collective-permute-start | bytes 2359304 | tf_op jit(solution)/shard_map/ppermute | solution.py:50
  114.7 49.5 %collective-permute-start.20 = (bf16[2,64,3072]{2,1,0:T(8,128)(2,1)S(1)}, bf16[2,64,3072]{2,1,0:T(8,128)(2,1)S(1)}, u32[]{:S(2)}, u32[]{:S(2)}) collective-permute-start(bf16[2,64,3072]{2,1,0:T(8,128)(2,1)S(1)} %dynamic-slice_bitcast_fusion.7), channel_id=1, source_target_pairs={{0,16},{8,24},{16,0},{24,8},{1,17},{9,25},{17,1},{25,9},{2,18},{10... | collective-permute-start | bytes 2359304 | tf_op jit(solution)/shard_map/ppermute | solution.py:50
  130.5 50.6 %collective-permute-start.8 = (bf16[2,64,3072]{2,1,0:T(8,128)(2,1)S(1)}, bf16[2,64,3072]{2,1,0:T(8,128)(2,1)S(1)}, u32[]{:S(2)}, u32[]{:S(2)}) collective-permute-start(bf16[2,64,3072]{2,1,0:T(8,128)(2,1)S(1)} %dynamic-slice_bitcast_fusion.10), channel_id=1, source_target_pairs={{0,16},{8,24},{16,0},{24,8},{1,17},{9,25},{17,1},{25,9},{2,18},{10... | collective-permute-start | bytes 2359304 | tf_op jit(solution)/shard_map/ppermute | solution.py:50
  147.3 35.5 %collective-permute-start.4 = (bf16[2,64,3072]{2,1,0:T(8,128)(2,1)S(1)}, bf16[2,64,3072]{2,1,0:T(8,128)(2,1)S(1)}, u32[]{:S(2)}, u32[]{:S(2)}) collective-permute-start(bf16[2,64,3072]{2,1,0:T(8,128)(2,1)S(1)} %dynamic-slice_bitcast_fusion.11), channel_id=1, source_target_pairs={{0,8},{8,0},{16,24},{24,16},{1,9},{9,1},{17,25},{25,17},{2,10},{10... | collective-permute-start | bytes 2359304 | tf_op jit(solution)/shard_map/ppermute | solution.py:50
  149.1 35.6 %collective-permute-start.16 = (bf16[2,64,3072]{2,1,0:T(8,128)(2,1)S(1)}, bf16[2,64,3072]{2,1,0:T(8,128)(2,1)S(1)}, u32[]{:S(2)}, u32[]{:S(2)}) collective-permute-start(bf16[2,64,3072]{2,1,0:T(8,128)(2,1)S(1)} %dynamic-slice_bitcast_fusion.8), channel_id=1, source_target_pairs={{0,8},{8,0},{16,24},{24,16},{1,9},{9,1},{17,25},{25,17},{2,10},{10... | collective-permute-start | bytes 2359304 | tf_op jit(solution)/shard_map/ppermute | solution.py:50
  149.9 43.1 %collective-permute-start.49 = (bf16[64,3072]{1,0:T(8,128)(2,1)S(1)}, bf16[64,3072]{1,0:T(8,128)(2,1)S(1)}, u32[]{:S(2)}, u32[]{:S(2)}) collective-permute-start(bf16[64,3072]{1,0:T(8,128)(2,1)S(1)} %dynamic-slice_bitcast_fusion.12), channel_id=1, source_target_pairs={{0,8},{8,0},{16,24},{24,16},{1,9},{9,1},{17,25},{25,17},{2,10},{10... | collective-permute-start | bytes 1179656 | tf_op jit(solution)/shard_map/ppermute | solution.py:50
  164.2 30.3 %collective-permute-start.45 = (bf16[64,3072]{1,0:T(8,128)(2,1)S(1)}, bf16[64,3072]{1,0:T(8,128)(2,1)S(1)}, u32[]{:S(2)}, u32[]{:S(2)}) collective-permute-start(bf16[64,3072]{1,0:T(8,128)(2,1)S(1)} %dynamic-slice_bitcast_fusion.13), channel_id=1, source_target_pairs={{0,16},{8,24},{16,0},{24,8},{1,17},{9,25},{17,1},{25,9},{2,18},{10... | collective-permute-start | bytes 1179656 | tf_op jit(solution)/shard_map/ppermute | solution.py:50
  181.0 20.4 %collective-permute-start.37 = (bf16[64,3072]{1,0:T(8,128)(2,1)S(1)}, bf16[64,3072]{1,0:T(8,128)(2,1)S(1)}, u32[]{:S(2)}, u32[]{:S(2)}) collective-permute-start(bf16[64,3072]{1,0:T(8,128)(2,1)S(1)} %dynamic-slice_bitcast_fusion.14), channel_id=1, source_target_pairs={{0,8},{8,0},{16,24},{24,16},{1,9},{9,1},{17,25},{25,17},{2,10},{10... | collective-permute-start | bytes 1179656 | tf_op jit(solution)/shard_map/ppermute | solution.py:50
  182.9 20.1 %collective-permute-start.33 = (bf16[64,3072]{1,0:T(8,128)(2,1)S(1)}, bf16[64,3072]{1,0:T(8,128)(2,1)S(1)}, u32[]{:S(2)}, u32[]{:S(2)}) collective-permute-start(bf16[64,3072]{1,0:T(8,128)(2,1)S(1)} %dynamic-slice_bitcast_fusion.15), channel_id=1, source_target_pairs={{0,16},{8,24},{16,0},{24,8},{1,17},{9,25},{17,1},{25,9},{2,18},{10... | collective-permute-start | bytes 1179656 | tf_op jit(solution)/shard_map/ppermute | solution.py:50
  184.6 37.4 %collective-permute-start.21 = (bf16[64,3072]{1,0:T(8,128)(2,1)S(1)}, bf16[64,3072]{1,0:T(8,128)(2,1)S(1)}, u32[]{:S(2)}, u32[]{:S(2)}) collective-permute-start(bf16[64,3072]{1,0:T(8,128)(2,1)S(1)} %dynamic-slice_bitcast_fusion.16), channel_id=1, source_target_pairs={{0,8},{8,0},{16,24},{24,16},{1,9},{9,1},{17,25},{25,17},{2,10},{10... | collective-permute-start | bytes 1179656 | tf_op jit(solution)/shard_map/ppermute | solution.py:50
  193.0 25.3 %collective-permute-start.9 = (bf16[64,3072]{1,0:T(8,128)(2,1)S(1)}, bf16[64,3072]{1,0:T(8,128)(2,1)S(1)}, u32[]{:S(2)}, u32[]{:S(2)}) collective-permute-start(bf16[64,3072]{1,0:T(8,128)(2,1)S(1)} %dynamic-slice_bitcast_fusion.18), channel_id=1, source_target_pairs={{0,8},{8,0},{16,24},{24,16},{1,9},{9,1},{17,25},{25,17},{2,10},{10... | collective-permute-start | bytes 1179656 | tf_op jit(solution)/shard_map/ppermute | solution.py:50
  194.5 25.3 %collective-permute-start.5 = (bf16[64,3072]{1,0:T(8,128)(2,1)S(1)}, bf16[64,3072]{1,0:T(8,128)(2,1)S(1)}, u32[]{:S(2)}, u32[]{:S(2)}) collective-permute-start(bf16[64,3072]{1,0:T(8,128)(2,1)S(1)} %dynamic-slice_bitcast_fusion.19), channel_id=1, source_target_pairs={{0,16},{8,24},{16,0},{24,8},{1,17},{9,25},{17,1},{25,9},{2,18},{10... | collective-permute-start | bytes 1179656 | tf_op jit(solution)/shard_map/ppermute | solution.py:50
  201.4 21.2 %collective-permute-start.17 = (bf16[64,3072]{1,0:T(8,128)(2,1)S(1)}, bf16[64,3072]{1,0:T(8,128)(2,1)S(1)}, u32[]{:S(2)}, u32[]{:S(2)}) collective-permute-start(bf16[64,3072]{1,0:T(8,128)(2,1)S(1)} %dynamic-slice_bitcast_fusion.17), channel_id=1, source_target_pairs={{0,16},{8,24},{16,0},{24,8},{1,17},{9,25},{17,1},{25,9},{2,18},{10... | collective-permute-start | bytes 1179656 | tf_op jit(solution)/shard_map/ppermute | solution.py:50
  203.0 28.9 %collective-permute-start.50 = (bf16[1,64,3072]{2,1,0:T(8,128)(2,1)S(1)}, bf16[1,64,3072]{2,1,0:T(8,128)(2,1)S(1)}, u32[]{:S(2)}, u32[]{:S(2)}) collective-permute-start(bf16[1,64,3072]{2,1,0:T(8,128)(2,1)S(1)} %get-tuple-element.28), channel_id=1, source_target_pairs={{0,8},{8,0},{16,24},{24,16},{1,9},{9,1},{17,25},{25,17},{2,10},{10... | collective-permute-start | bytes 1179656 | tf_op jit(solution)/shard_map/ppermute | solution.py:50
  219.8 20.5 %collective-permute-start.38 = (bf16[1,64,3072]{2,1,0:T(8,128)(2,1)S(1)}, bf16[1,64,3072]{2,1,0:T(8,128)(2,1)S(1)}, u32[]{:S(2)}, u32[]{:S(2)}) collective-permute-start(bf16[1,64,3072]{2,1,0:T(8,128)(2,1)S(1)} %get-tuple-element.26), channel_id=1, source_target_pairs={{0,8},{8,0},{16,24},{24,16},{1,9},{9,1},{17,25},{25,17},{2,10},{10... | collective-permute-start | bytes 1179656 | tf_op jit(solution)/shard_map/ppermute | solution.py:50
  222.0 16.7 %collective-permute-start.34 = (bf16[1,64,3072]{2,1,0:T(8,128)(2,1)S(1)}, bf16[1,64,3072]{2,1,0:T(8,128)(2,1)S(1)}, u32[]{:S(2)}, u32[]{:S(2)}) collective-permute-start(bf16[1,64,3072]{2,1,0:T(8,128)(2,1)S(1)} %get-tuple-element.27), channel_id=1, source_target_pairs={{0,16},{8,24},{16,0},{24,8},{1,17},{9,25},{17,1},{25,9},{2,18},{10... | collective-permute-start | bytes 1179656 | tf_op jit(solution)/shard_map/ppermute | solution.py:50
  222.6 26.1 %collective-permute-start.10 = (bf16[1,64,3072]{2,1,0:T(8,128)(2,1)S(1)}, bf16[1,64,3072]{2,1,0:T(8,128)(2,1)S(1)}, u32[]{:S(2)}, u32[]{:S(2)}) collective-permute-start(bf16[1,64,3072]{2,1,0:T(8,128)(2,1)S(1)} %get-tuple-element.22), channel_id=1, source_target_pairs={{0,8},{8,0},{16,24},{24,16},{1,9},{9,1},{17,25},{25,17},{2,10},{10... | collective-permute-start | bytes 1179656 | tf_op jit(solution)/shard_map/ppermute | solution.py:50
  230.3 16.9 %collective-permute-start.6 = (bf16[1,64,3072]{2,1,0:T(8,128)(2,1)S(1)}, bf16[1,64,3072]{2,1,0:T(8,128)(2,1)S(1)}, u32[]{:S(2)}, u32[]{:S(2)}) collective-permute-start(bf16[1,64,3072]{2,1,0:T(8,128)(2,1)S(1)} %get-tuple-element.23), channel_id=1, source_target_pairs={{0,16},{8,24},{16,0},{24,8},{1,17},{9,25},{17,1},{25,9},{2,18},{10... | collective-permute-start | bytes 1179656 | tf_op jit(solution)/shard_map/ppermute | solution.py:50
  231.9 25.3 %collective-permute-start.22 = (bf16[1,64,3072]{2,1,0:T(8,128)(2,1)S(1)}, bf16[1,64,3072]{2,1,0:T(8,128)(2,1)S(1)}, u32[]{:S(2)}, u32[]{:S(2)}) collective-permute-start(bf16[1,64,3072]{2,1,0:T(8,128)(2,1)S(1)} %get-tuple-element.24), channel_id=1, source_target_pairs={{0,8},{8,0},{16,24},{24,16},{1,9},{9,1},{17,25},{25,17},{2,10},{10... | collective-permute-start | bytes 1179656 | tf_op jit(solution)/shard_map/ppermute | solution.py:50
  238.7 16.9 %collective-permute-start.18 = (bf16[1,64,3072]{2,1,0:T(8,128)(2,1)S(1)}, bf16[1,64,3072]{2,1,0:T(8,128)(2,1)S(1)}, u32[]{:S(2)}, u32[]{:S(2)}) collective-permute-start(bf16[1,64,3072]{2,1,0:T(8,128)(2,1)S(1)} %get-tuple-element.25), channel_id=1, source_target_pairs={{0,16},{8,24},{16,0},{24,8},{1,17},{9,25},{17,1},{25,9},{2,18},{10... | collective-permute-start | bytes 1179656 | tf_op jit(solution)/shard_map/ppermute | solution.py:50
  240.3 92.3 %collective-permute-start.51 = (bf16[2,64,3072]{2,1,0:T(8,128)(2,1)S(1)}, bf16[2,64,3072]{2,1,0:T(8,128)(2,1)S(1)}, u32[]{:S(2)}, u32[]{:S(2)}) collective-permute-start(bf16[2,64,3072]{2,1,0:T(8,128)(2,1)S(1)} %pad_maximum_fusion.21), channel_id=1, source_target_pairs={{0,16},{8,24},{16,0},{24,8},{1,17},{9,25},{17,1},{25,9},{2,18},{10... | collective-permute-start | bytes 2359304 | tf_op jit(solution)/shard_map/ppermute | solution.py:50
  247.1 21.7 %collective-permute-start.47 = (bf16[2,64,3072]{2,1,0:T(8,128)(2,1)S(1)}, bf16[2,64,3072]{2,1,0:T(8,128)(2,1)S(1)}, u32[]{:S(2)}, u32[]{:S(2)}) collective-permute-start(bf16[2,64,3072]{2,1,0:T(8,128)(2,1)S(1)} %pad_maximum_fusion.20), channel_id=1, source_target_pairs={{0,8},{8,0},{16,24},{24,16},{1,9},{9,1},{17,25},{25,17},{2,10},{10... | collective-permute-start | bytes 2359304 | tf_op jit(solution)/shard_map/ppermute | solution.py:50
  248.7 90.7 %collective-permute-start.39 = (bf16[2,64,3072]{2,1,0:T(8,128)(2,1)S(1)}, bf16[2,64,3072]{2,1,0:T(8,128)(2,1)S(1)}, u32[]{:S(2)}, u32[]{:S(2)}) collective-permute-start(bf16[2,64,3072]{2,1,0:T(8,128)(2,1)S(1)} %pad_maximum_fusion.19), channel_id=1, source_target_pairs={{0,16},{8,24},{16,0},{24,8},{1,17},{9,25},{17,1},{25,9},{2,18},{10... | collective-permute-start | bytes 2359304 | tf_op jit(solution)/shard_map/ppermute | solution.py:50
  255.6 30.1 %collective-permute-start.35 = (bf16[2,64,3072]{2,1,0:T(8,128)(2,1)S(1)}, bf16[2,64,3072]{2,1,0:T(8,128)(2,1)S(1)}, u32[]{:S(2)}, u32[]{:S(2)}) collective-permute-start(bf16[2,64,3072]{2,1,0:T(8,128)(2,1)S(1)} %pad_maximum_fusion.18), channel_id=1, source_target_pairs={{0,8},{8,0},{16,24},{24,16},{1,9},{9,1},{17,25},{25,17},{2,10},{10... | collective-permute-start | bytes 2359304 | tf_op jit(solution)/shard_map/ppermute | solution.py:50
  257.1 42.7 %collective-permute-start.7 = (bf16[2,64,3072]{2,1,0:T(8,128)(2,1)S(1)}, bf16[2,64,3072]{2,1,0:T(8,128)(2,1)S(1)}, u32[]{:S(2)}, u32[]{:S(2)}) collective-permute-start(bf16[2,64,3072]{2,1,0:T(8,128)(2,1)S(1)} %pad_maximum_fusion.14), channel_id=1, source_target_pairs={{0,8},{8,0},{16,24},{24,16},{1,9},{9,1},{17,25},{25,17},{2,10},{10... | collective-permute-start | bytes 2359304 | tf_op jit(solution)/shard_map/ppermute | solution.py:50
  268.8 50.7 %collective-permute-start.11 = (bf16[2,64,3072]{2,1,0:T(8,128)(2,1)S(1)}, bf16[2,64,3072]{2,1,0:T(8,128)(2,1)S(1)}, u32[]{:S(2)}, u32[]{:S(2)}) collective-permute-start(bf16[2,64,3072]{2,1,0:T(8,128)(2,1)S(1)} %pad_maximum_fusion.15), channel_id=1, source_target_pairs={{0,16},{8,24},{16,0},{24,8},{1,17},{9,25},{17,1},{25,9},{2,18},{10... | collective-permute-start | bytes 2359304 | tf_op jit(solution)/shard_map/ppermute | solution.py:50
  285.7 41.0 %collective-permute-start.23 = (bf16[2,64,3072]{2,1,0:T(8,128)(2,1)S(1)}, bf16[2,64,3072]{2,1,0:T(8,128)(2,1)S(1)}, u32[]{:S(2)}, u32[]{:S(2)}) collective-permute-start(bf16[2,64,3072]{2,1,0:T(8,128)(2,1)S(1)} %pad_maximum_fusion.17), channel_id=1, source_target_pairs={{0,16},{8,24},{16,0},{24,8},{1,17},{9,25},{17,1},{25,9},{2,18},{10... | collective-permute-start | bytes 2359304 | tf_op jit(solution)/shard_map/ppermute | solution.py:50
  299.9 16.8 %collective-permute-start.19 = (bf16[2,64,3072]{2,1,0:T(8,128)(2,1)S(1)}, bf16[2,64,3072]{2,1,0:T(8,128)(2,1)S(1)}, u32[]{:S(2)}, u32[]{:S(2)}) collective-permute-start(bf16[2,64,3072]{2,1,0:T(8,128)(2,1)S(1)} %pad_maximum_fusion.16), channel_id=1, source_target_pairs={{0,8},{8,0},{16,24},{24,16},{1,9},{9,1},{17,25},{25,17},{2,10},{10... | collective-permute-start | bytes 2359304 | tf_op jit(solution)/shard_map/ppermute | solution.py:50
  348.4 21.8 %collective-permute-start.14 = (bf16[32,3072]{1,0:T(8,128)(2,1)S(1)}, bf16[32,3072]{1,0:T(8,128)(2,1)S(1)}, u32[]{:S(2)}, u32[]{:S(2)}) collective-permute-start(bf16[32,3072]{1,0:T(8,128)(2,1)S(1)} %get-tuple-element.34), channel_id=1, source_target_pairs={{0,4},{1,5},{2,6},{3,7},{4,0},{5,1},{6,2},{7,3},{8,12},{9,13},{10,... | collective-permute-start | bytes 589832 | tf_op jit(solution)/shard_map/ppermute | solution.py:54
  348.6 21.7 %collective-permute-start.25 = (bf16[32,3072]{1,0:T(8,128)(2,1)S(1)}, bf16[32,3072]{1,0:T(8,128)(2,1)S(1)}, u32[]{:S(2)}, u32[]{:S(2)}) collective-permute-start(bf16[32,3072]{1,0:T(8,128)(2,1)S(1)} %get-tuple-element.35), channel_id=1, source_target_pairs={{0,2},{1,3},{2,4},{3,5},{4,6},{5,7},{6,0},{7,1},{8,10},{9,11},{10,... | collective-permute-start | bytes 589832 | tf_op jit(solution)/shard_map/ppermute | solution.py:54
  349.7 27.8 %collective-permute-start.27 = (bf16[32,3072]{1,0:T(8,128)(2,1)S(1)}, bf16[32,3072]{1,0:T(8,128)(2,1)S(1)}, u32[]{:S(2)}, u32[]{:S(2)}) collective-permute-start(bf16[32,3072]{1,0:T(8,128)(2,1)S(1)} %get-tuple-element.36), channel_id=1, source_target_pairs={{0,6},{1,7},{2,0},{3,1},{4,2},{5,3},{6,4},{7,5},{8,14},{9,15},{10,... | collective-permute-start | bytes 589832 | tf_op jit(solution)/shard_map/ppermute | solution.py:54
  354.2 40.8 %collective-permute-start.26 = (bf16[32,3072]{1,0:T(8,128)(2,1)S(1)}, bf16[32,3072]{1,0:T(8,128)(2,1)S(1)}, u32[]{:S(2)}, u32[]{:S(2)}) collective-permute-start(bf16[32,3072]{1,0:T(8,128)(2,1)S(1)} %get-tuple-element.37), channel_id=1, source_target_pairs={{0,4},{1,5},{2,6},{3,7},{4,0},{5,1},{6,2},{7,3},{8,12},{9,13},{10,... | collective-permute-start | bytes 589832 | tf_op jit(solution)/shard_map/ppermute | solution.py:54
  358.1 37.0 %collective-permute-start.41 = (bf16[32,3072]{1,0:T(8,128)(2,1)S(1)}, bf16[32,3072]{1,0:T(8,128)(2,1)S(1)}, u32[]{:S(2)}, u32[]{:S(2)}) collective-permute-start(bf16[32,3072]{1,0:T(8,128)(2,1)S(1)} %get-tuple-element.38), channel_id=1, source_target_pairs={{0,2},{1,3},{2,4},{3,5},{4,6},{5,7},{6,0},{7,1},{8,10},{9,11},{10,... | collective-permute-start | bytes 589832 | tf_op jit(solution)/shard_map/ppermute | solution.py:54
  370.2 25.0 %collective-permute-start.43 = (bf16[32,3072]{1,0:T(8,128)(2,1)S(1)}, bf16[32,3072]{1,0:T(8,128)(2,1)S(1)}, u32[]{:S(2)}, u32[]{:S(2)}) collective-permute-start(bf16[32,3072]{1,0:T(8,128)(2,1)S(1)} %get-tuple-element.39), channel_id=1, source_target_pairs={{0,6},{1,7},{2,0},{3,1},{4,2},{5,3},{6,4},{7,5},{8,14},{9,15},{10,... | collective-permute-start | bytes 589832 | tf_op jit(solution)/shard_map/ppermute | solution.py:54
  370.3 37.3 %collective-permute-start.42 = (bf16[32,3072]{1,0:T(8,128)(2,1)S(1)}, bf16[32,3072]{1,0:T(8,128)(2,1)S(1)}, u32[]{:S(2)}, u32[]{:S(2)}) collective-permute-start(bf16[32,3072]{1,0:T(8,128)(2,1)S(1)} %get-tuple-element.40), channel_id=1, source_target_pairs={{0,4},{1,5},{2,6},{3,7},{4,0},{5,1},{6,2},{7,3},{8,12},{9,13},{10,... | collective-permute-start | bytes 589832 | tf_op jit(solution)/shard_map/ppermute | solution.py:54
  377.5 31.9 %collective-permute-start.53 = (bf16[32,3072]{1,0:T(8,128)(2,1)S(1)}, bf16[32,3072]{1,0:T(8,128)(2,1)S(1)}, u32[]{:S(2)}, u32[]{:S(2)}) collective-permute-start(bf16[32,3072]{1,0:T(8,128)(2,1)S(1)} %get-tuple-element.41), channel_id=1, source_target_pairs={{0,2},{1,3},{2,4},{3,5},{4,6},{5,7},{6,0},{7,1},{8,10},{9,11},{10,... | collective-permute-start | bytes 589832 | tf_op jit(solution)/shard_map/ppermute | solution.py:54
  395.0 14.5 %collective-permute-start.55 = (bf16[32,3072]{1,0:T(8,128)(2,1)S(1)}, bf16[32,3072]{1,0:T(8,128)(2,1)S(1)}, u32[]{:S(2)}, u32[]{:S(2)}) collective-permute-start(bf16[32,3072]{1,0:T(8,128)(2,1)S(1)} %get-tuple-element.42), channel_id=1, source_target_pairs={{0,6},{1,7},{2,0},{3,1},{4,2},{5,3},{6,4},{7,5},{8,14},{9,15},{10,... | collective-permute-start | bytes 589832 | tf_op jit(solution)/shard_map/ppermute | solution.py:54
  395.1 20.0 %collective-permute-start.54 = (bf16[32,3072]{1,0:T(8,128)(2,1)S(1)}, bf16[32,3072]{1,0:T(8,128)(2,1)S(1)}, u32[]{:S(2)}, u32[]{:S(2)}) collective-permute-start(bf16[32,3072]{1,0:T(8,128)(2,1)S(1)} %get-tuple-element.43), channel_id=1, source_target_pairs={{0,4},{1,5},{2,6},{3,7},{4,0},{5,1},{6,2},{7,3},{8,12},{9,13},{10,... | collective-permute-start | bytes 589832 | tf_op jit(solution)/shard_map/ppermute | solution.py:54
  (26 other events, 296.2 us)
